TPU v7x, 256 devices: a whole 4x4x8 slice. The times are simulated.
256 devices in a mesh: blk: 16 (over z, core), head: 4 (over x), dp: 4 (over y).
Axes of the slice: x: 4, y: 4, z: 8, core: 2. Of those that a mesh axis runs over, the one named last changes fastest.
Arguments:
- hidden: bfloat16 [49152, 3072], P(('dp', 'blk', 'head')), parts along dimension 0, may hold values from -36 to 36
- qkv_weight: bfloat16 [3, 3072, 1536], P(None, None, 'head'), may hold values from -0.109375 to 0.109375
- qkv_bias: bfloat16 [3, 1536], P(None, 'head'), may hold values from -3 to 3
- norm_gains: float32 [2, 128], replicated, may hold values from 0.25 to 1.75
- tile_lists: int32 [128, 12], P('dp'), parts along dimension 0, may hold values from 0 to 31, as said below
- tile_counts: int32 [128], P('dp'), parts along dimension 0, may hold values from 1 to 12
Outputs:
- attended: bfloat16 [49152, 1536], P(('dp', 'blk', 'head')), parts along dimension 0
There are 4 independent parts, one for each index of `dp`. A program takes and returns all parts, laid end to end along the dimension named above; an argument that names none is the same for every part. Nothing has to cross between parts.
Inputs may be any that keep to these rules, and one draw needn't show every extreme that they name: `tile_lists`: entries 0 to tile_counts[a] - 1 of row a name distinct tiles, tile a among them; later entries are arbitrary tile indices.
All inputs are finite; a program needn't handle non-finite values.
Results may differ from a plain program's by a relative error of at most 0.0034.
Values may be sent and summed in bfloat16 or wider, within the bound.
A program may use at most 64 MiB of HBM per device.

v0:
```python
import jax
import jax.numpy as jnp
from jax import lax
from jax.sharding import PartitionSpec as P

HD = 128
TILE = 384


def shifted(block, axis, distance):
    devices = range(lax.axis_size(axis))
    route = [(i - distance, i) for i in devices if i - distance in devices]
    return lax.ppermute(block, axis, route)


def norm_heads(values, gain, heads):
    rows = values.shape[0]
    split = values.reshape(rows, heads, HD)
    mean_sq = jnp.mean(split * split, axis=-1, keepdims=True)
    return (split * lax.rsqrt(mean_sq + 1e-06) * gain).reshape(rows, heads * HD)


def tile_mask(lists, counts, start, rows):
    key_tile = (start + jnp.arange(rows, dtype=jnp.int32)) // TILE
    live = jnp.arange(lists.shape[1], dtype=jnp.int32)[None, :] < counts[:, None]
    hits = (lists[:, :, None] == key_tile[None, None, :]) & live[:, :, None]
    return jnp.any(hits, axis=1)


def tile_terms(query, keys, values, mask, heads):
    count_q = query.shape[0]
    rows = keys.shape[0]
    query_h = query.reshape(count_q, heads, HD)
    keys_h = keys.reshape(rows, heads, HD)
    values_h = values.reshape(rows, heads, HD)
    score = jnp.einsum(
        "qhd,khd->hqk", query_h, keys_h, preferred_element_type=jnp.float32
    ) * HD ** (-0.5)
    score = score.reshape(heads, count_q // TILE, TILE, rows)
    weights = jnp.where(mask[None, :, None, :], jnp.exp(score), jnp.float32(0.0)).reshape(
        heads, count_q, rows
    )
    sums = jnp.sum(weights, axis=-1)
    terms = jnp.einsum(
        "hqk,khd->qhd", weights.astype(jnp.bfloat16), values_h, preferred_element_type=jnp.float32
    )
    return (sums, terms.reshape(count_q, heads * HD))


def add_block(state, query, lists, counts, keys, values, start, heads):
    total, numer = state
    mask = tile_mask(lists, counts, start, keys.shape[0])
    sums, terms = tile_terms(query, keys, values, mask, heads)
    return (total + sums, numer + terms)


def attend(state, query, lists, counts, keys, values, start, heads):
    return add_block(state, query, lists, counts, keys, values, start, heads)


def shards(hidden, qkv_weight, qkv_bias, norm_gains, tile_lists, tile_counts):
    heads = qkv_weight.shape[2] // HD
    piece = lax.all_gather(hidden, "head", axis=0, tiled=True)
    made = [
        jnp.dot(piece, qkv_weight[j], preferred_element_type=jnp.float32)
        + qkv_bias[j].astype(jnp.float32)
        for j in range(3)
    ]
    query_part = norm_heads(made[0], norm_gains[0], heads)
    key_part = norm_heads(made[1], norm_gains[1], heads)
    stacked = jnp.stack([query_part, key_part, made[2]]).astype(jnp.bfloat16)
    query = stacked[0]
    key_value = stacked[1:3]
    rows_blk = query.shape[0]
    tiles_here = rows_blk // TILE
    place = lax.axis_index("blk")
    lists = lax.dynamic_slice_in_dim(tile_lists, place * tiles_here, tiles_here, 0)
    counts = lax.dynamic_slice_in_dim(tile_counts, place * tiles_here, tiles_here, 0)
    state = (
        jnp.zeros((heads, rows_blk), jnp.float32),
        jnp.zeros((rows_blk, heads * HD), jnp.float32),
    )
    key_group = lists // tiles_here
    live = jnp.arange(lists.shape[1], dtype=jnp.int32)[None, :] < counts[:, None]
    ahead = jnp.max(jnp.where(live, key_group - place, 0))
    behind = jnp.max(jnp.where(live, place - key_group, 0))
    farthest = lax.pmax(jnp.stack([ahead, behind]), "blk")
    state = attend(state, query, lists, counts, key_value[0], key_value[1], place * rows_blk, heads)

    def turn(step, carry):
        current, above, below = carry
        above = shifted(above, "blk", -1)
        below = shifted(below, "blk", 1)
        current = attend(
            current, query, lists, counts, above[0], above[1], (place + step + 1) * rows_blk, heads
        )
        current = attend(
            current, query, lists, counts, below[0], below[1], (place - step - 1) * rows_blk, heads
        )
        return (current, above, below)

    steps = jnp.maximum(farthest[0], farthest[1])
    state, unused_above, unused_below = lax.fori_loop(0, steps, turn, (state, key_value, key_value))
    total, numer = state
    attended = (
        (numer.reshape(rows_blk, heads, HD) / total.T[:, :, None])
        .reshape(rows_blk, heads * HD)
        .astype(jnp.bfloat16)
    )
    return lax.all_to_all(attended, "head", split_axis=0, concat_axis=1, tiled=True)


def solution(mesh):
    return jax.shard_map(
        shards,
        mesh=mesh,
        in_specs=(
            P(("dp", "blk", "head"), None),
            P(None, None, "head"),
            P(None, "head"),
            P(),
            P("dp", None),
            P("dp"),
        ),
        out_specs=P(("dp", "blk", "head"), None),
        check_vma=False,
    )
```

profile of v0, /device:TPU:65, one launch (start us, length us, event | category | flops | bytes accessed | tf_op | source)
XLA Modules:
  0.0 199.9 jit_solution(13299230233405282443)
XLA Ops:
  10.2 12.0 %pmax.7 = s32[2]{0:T(128)S(1)} all-reduce(s32[2]{0:T(128)S(1)} %pad_add_fusion), channel_id=1, replica_groups=mesh['blk'=16,'head'=4,'dp'=4] {'blk'}, use_global_device_ids=true, to_apply=%region_6.7 | all-reduce | flops 2 | bytes 16 | tf_op jit(solution)/shard_map/pmax | solution.py:87
  22.6 1.6 copy.56
  27.2 39.2 %all-gather.2.cloned.1.call-done = bf16[768,3072]{1,0:T(8,128)(2,1)} async-done(((bf16[192,3072]{1,0:T(8,128)(2,1)}), bf16[768,3072]{1,0:T(8,128)(2,1)}) %all-gather.2.cloned.1.call-update) | async-done | bytes 4718608 | tf_op jit(solution)/shard_map/all_gather | solution.py:63
  66.3 5.1 %fusion.60 = (f32[768,384]{0,1:T(8,128)S(1)}, f32[768,384]{0,1:T(8,128)S(1)}) fusion(f32[384]{0:T(512)S(1)} %get-tuple-element.181, bf16[768,3072]{1,0:T(8,128)(2,1)} %all-gather.2.cloned.1.call-done, bf16[3,3072,384]{2,1,0:T(8,128)(2,1)} %param.9), kind=kOutput, calls=%fused_computation.93 | convolution fusion | flops 1812529152 | bytes 9438720 | tf_op jit(solution)/shard_map/dot_general | solution.py:65
  72.2 5.1 %fusion.59 = (f32[768,384]{0,1:T(8,128)S(1)}, f32[768,384]{0,1:T(8,128)S(1)}) fusion(f32[384]{0:T(512)} %get-tuple-element.180, bf16[768,3072]{1,0:T(8,128)(2,1)} %all-gather.2.cloned.1.call-done, bf16[3,3072,384]{2,1,0:T(8,128)(2,1)} %param.9), kind=kOutput, calls=%fused_computation.92 | convolution fusion | flops 1812529152 | bytes 9439232 | tf_op jit(solution)/shard_map/dot_general | solution.py:65
  79.6 5.1 %fusion.45 = bf16[768,384]{0,1:T(8,128)(2,1)S(1)} fusion(bf16[768,3072]{1,0:T(8,128)(2,1)} %all-gather.2.cloned.1.call-done, bf16[3,3072,384]{2,1,0:T(8,128)(2,1)} %param.9, f32[384]{0:T(512)} %get-tuple-element.179), kind=kOutput, calls=%fused_computation.53 | convolution fusion | flops 1812529152 | bytes 7669760 | tf_op jit(solution)/shard_map/dot_general | solution.py:65
  85.8 2.5 %copy.81 = bf16[2,768,384]{1,2,0:T(8,128)(2,1)} copy(bf16[2,768,384]{1,2,0:T(8,128)(2,1)} %pad_maximum_fusion) | data formatting | bytes 2359296
  88.4 2.5 %fusion.21 = (f32[3,768]{1,0:T(4,128)}, f32[3,768,768]{1,2,0:T(8,128)S(1)}) fusion(pred[768,768]{0,1:T(8,128)(4,1)S(1)} %copy-done.4, bf16[768,3,128]{0,2,1:T(8,128)(2,1)S(1)} %bitcast.138, bf16[768,3,128]{0,2,1:T(8,128)(2,1)S(1)} %bitcast.135), kind=kOutput, calls=%fused_computation.36 | convolution fusion | flops 458290944 | bytes 8856576 | tf_op jit(solution)/shard_map/qhd,khd->hqk/dot_general | solution.py:36
  91.0 2.6 %fusion.22 = f32[3,128,768]{2,1,0:T(8,128)} fusion(bf16[768,3,128]{0,2,1:T(8,128)(2,1)S(1)} %bitcast.143, f32[3,768,768]{1,2,0:T(8,128)S(1)} %get-tuple-element.223, pred[768,768]{0,1:T(8,128)(4,1)S(1)} %copy-done.4), kind=kOutput, calls=%fused_computation.37 | convolution fusion | flops 458293248 | bytes 9437184 | tf_op jit(solution)/shard_map/hqk,khd->qhd/dot_general | solution.py:44
  93.5 84.3 %while.19 = (s32[]{:T(128)}, f32[3,768]{1,0:T(4,128)}, f32[768,384]{0,1:T(8,128)}, bf16[2,768,384]{1,2,0:T(8,128)(2,1)}, bf16[2,768,384]{1,2,0:T(8,128)(2,1)}, /...) while((s32[]{:T(128)}, f32[3,768]{1,0:T(4,128)}, ...), condition=%wide.region_12.13_spmd, body=%wide.region_7.12_spmd.sunk | while | flops 1833884160 | bytes 78004824 | solution.py:103
  93.5 2.7 %collective-permute-start.1 = (bf16[2,768,384]{1,2,0:T(8,128)(2,1)}, bf16[2,768,384]{1,2,0:T(8,128)(2,1)S(1)}, u32[]{:S(2)}, u32[]{:S(2)}) collective-permute-start(bf16[2,768,384]{1,2,0:T(8,128)(2,1)} %get-tuple-element.328), channel_id=1, source_target_pairs={{16,0},{32,16},{48,32},{64,48},{80,64},{96,80},{112,96},{128,112},... | collective-permute-start | bytes 3538952 | tf_op jit(solution)/shard_map/while/body/ppermute | solution.py:13
  96.3 3.1 %collective-permute-start = (bf16[2,768,384]{1,2,0:T(8,128)(2,1)}, bf16[2,768,384]{1,2,0:T(8,128)(2,1)S(1)}, u32[]{:S(2)}, u32[]{:S(2)}) collective-permute-start(bf16[2,768,384]{1,2,0:T(8,128)(2,1)} %get-tuple-element.329), channel_id=1, source_target_pairs={{0,16},{16,32},{32,48},{48,64},{64,80},{80,96},{96,112},{112,128},... | collective-permute-start | bytes 3538952 | tf_op jit(solution)/shard_map/while/body/ppermute | solution.py:13
  99.8 1.6 copy.76
  102.5 9.3 %collective-permute-done.1 = bf16[2,768,384]{1,2,0:T(8,128)(2,1)S(1)} collective-permute-done((bf16[2,768,384]{1,2,0:T(8,128)(2,1)}, bf16[2,768,384]{1,2,0:T(8,128)(2,1)S(1)}, u32[]{:S(2)}, u32[]{:S(2)}) %collective-permute-start.1) | collective-permute-done | bytes 1179680 | tf_op jit(solution)/shard_map/while/body/ppermute | solution.py:13
  111.9 1.9 fusion.98
  113.8 1.6 fusion.100
  115.5 1.9 fusion.96
  121.8 1.9 collective-permute-start.1
  123.7 3.6 %collective-permute-start = (bf16[2,768,384]{1,2,0:T(8,128)(2,1)}, bf16[2,768,384]{1,2,0:T(8,128)(2,1)S(1)}, u32[]{:S(2)}, u32[]{:S(2)}) collective-permute-start(bf16[2,768,384]{1,2,0:T(8,128)(2,1)} %get-tuple-element.329), channel_id=1, source_target_pairs={{0,16},{16,32},{32,48},{48,64},{64,80},{80,96},{96,112},{112,128},... | collective-permute-start | bytes 3538952 | tf_op jit(solution)/shard_map/while/body/ppermute | solution.py:13
  127.8 1.6 copy.76
  130.6 9.3 %collective-permute-done.1 = bf16[2,768,384]{1,2,0:T(8,128)(2,1)S(1)} collective-permute-done((bf16[2,768,384]{1,2,0:T(8,128)(2,1)}, bf16[2,768,384]{1,2,0:T(8,128)(2,1)S(1)}, u32[]{:S(2)}, u32[]{:S(2)}) %collective-permute-start.1) | collective-permute-done | bytes 1179680 | tf_op jit(solution)/shard_map/while/body/ppermute | solution.py:13
  139.9 1.9 fusion.98
  141.9 1.6 fusion.100
  143.6 1.9 fusion.96
  149.8 1.9 collective-permute-start.1
  151.8 3.6 %collective-permute-start = (bf16[2,768,384]{1,2,0:T(8,128)(2,1)}, bf16[2,768,384]{1,2,0:T(8,128)(2,1)S(1)}, u32[]{:S(2)}, u32[]{:S(2)}) collective-permute-start(bf16[2,768,384]{1,2,0:T(8,128)(2,1)} %get-tuple-element.329), channel_id=1, source_target_pairs={{0,16},{16,32},{32,48},{48,64},{64,80},{80,96},{96,112},{112,128},... | collective-permute-start | bytes 3538952 | tf_op jit(solution)/shard_map/while/body/ppermute | solution.py:13
  155.8 1.6 copy.76
  158.6 9.3 %collective-permute-done.1 = bf16[2,768,384]{1,2,0:T(8,128)(2,1)S(1)} collective-permute-done((bf16[2,768,384]{1,2,0:T(8,128)(2,1)}, bf16[2,768,384]{1,2,0:T(8,128)(2,1)S(1)}, u32[]{:S(2)}, u32[]{:S(2)}) %collective-permute-start.1) | collective-permute-done | bytes 1179680 | tf_op jit(solution)/shard_map/while/body/ppermute | solution.py:13
  168.0 1.9 fusion.98
  169.9 1.6 fusion.100
  171.6 1.9 fusion.96
  179.5 12.7 %all_to_all.19 = bf16[4,192,384]{2,1,0:T(8,128)(2,1)S(1)} all-to-all(bf16[4,192,384]{2,1,0:T(8,128)(2,1)S(1)} %bitcast.132), channel_id=1, replica_groups=mesh['blk'=16,'head'=4,'dp'=4] {'head'}, dimensions={0} | all-to-all | bytes 1179648 | tf_op jit(solution)/shard_map/all_to_all | solution.py:110
  (117 shorter events, 30.7 us)
Async XLA Ops:
  6.5 0.7 copy-start
  6.5 19.4 %copy-start.9 = (bf16[3,384]{1,0:T(4,128)(2,1)S(1)}, bf16[3,384]{1,0:T(4,128)(2,1)}, u32[]{:S(2)}) copy-start(bf16[3,384]{1,0:T(4,128)(2,1)} %param.10) | copy-start | bytes 6916
  6.5 20.1 %copy-start.10 = (f32[2,128]{1,0:T(2,128)S(1)}, f32[2,128]{1,0:T(2,128)}, u32[]{:S(2)}) copy-start(f32[2,128]{1,0:T(2,128)} %param.11) | copy-start | bytes 3076
  6.5 59.8 %all-gather.2.cloned.1.call-start = ((), (), s32[]{:S(2)}) async-start(), calls=%async_computation.1 | async-start | bytes 5898240 | tf_op jit(solution)/shard_map/all_gather | solution.py:63
  8.2 14.2 %copy-start.11 = (s32[2]{0:T(128)}, s32[2]{0:T(128)S(1)}, u32[]{:S(2)}) copy-start(s32[2]{0:T(128)S(1)} %dynamic_slice.7) | copy-start | bytes 28
  85.8 2.7 %copy-start.4 = (pred[768,768]{0,1:T(8,128)(4,1)S(1)}, pred[768,768]{0,1:T(8,128)(4,1)}, u32[]{:S(2)}) copy-start(pred[768,768]{0,1:T(8,128)(4,1)} %copy.56) | copy-start | bytes 1769476
  88.4 2.5 %copy-start.5 = (bf16[768,384]{0,1:T(8,128)(2,1)}, bf16[768,384]{0,1:T(8,128)(2,1)S(1)}, u32[]{:S(2)}) copy-start(bf16[768,384]{0,1:T(8,128)(2,1)S(1)} %fusion.52) | copy-start | bytes 1769476
  91.0 2.6 %copy-start.12 = (s32[2]{0:T(128)S(1)}, s32[2]{0:T(128)}, u32[]{:S(2)}) copy-start(s32[2]{0:T(128)} %copy-done.11) | copy-start | bytes 28
  93.5 18.3 %collective-permute-start.1 = (bf16[2,768,384]{1,2,0:T(8,128)(2,1)}, bf16[2,768,384]{1,2,0:T(8,128)(2,1)S(1)}, u32[]{:S(2)}, u32[]{:S(2)}) collective-permute-start(bf16[2,768,384]{1,2,0:T(8,128)(2,1)} %get-tuple-element.328), channel_id=1, source_target_pairs={{16,0},{32,16},{48,32},{64,48},{80,64},{96,80},{112,96},{128,112},... | collective-permute-start | bytes 3538952 | tf_op jit(solution)/shard_map/while/body/ppermute | solution.py:13
  96.3 19.2 %collective-permute-start = (bf16[2,768,384]{1,2,0:T(8,128)(2,1)}, bf16[2,768,384]{1,2,0:T(8,128)(2,1)S(1)}, u32[]{:S(2)}, u32[]{:S(2)}) collective-permute-start(bf16[2,768,384]{1,2,0:T(8,128)(2,1)} %get-tuple-element.329), channel_id=1, source_target_pairs={{0,16},{16,32},{32,48},{48,64},{64,80},{80,96},{96,112},{112,128},... | collective-permute-start | bytes 3538952 | tf_op jit(solution)/shard_map/while/body/ppermute | solution.py:13
  102.5 9.4 %copy-start.3 = (pred[768,768]{0,1:T(8,128)(4,1)S(1)}, pred[768,768]{0,1:T(8,128)(4,1)}, u32[]{:S(2)}) copy-start(pred[768,768]{0,1:T(8,128)(4,1)} %copy.76) | copy-start | bytes 1769476 | tf_op jit(solution)/shard_map/while
  102.5 9.4 %copy-start.6 = (bf16[1,768,384]{1,2,0:T(8,128)(2,1)S(1)}, bf16[1,768,384]{1,2,0:T(8,128)(2,1)}, u32[]{:S(2)}) copy-start(bf16[1,768,384]{1,2,0:T(8,128)(2,1)} %get-tuple-element.347) | copy-start | bytes 1769476 | tf_op jit(solution)/shard_map/while
  117.4 1.6 copy-start.1
  119.0 0.7 copy-start.7
  119.4 2.5 %copy-start.2 = (f32[768,384]{0,1:T(8,128)}, f32[768,384]{0,1:T(8,128)S(1)}, u32[]{:S(2)}) copy-start(f32[768,384]{0,1:T(8,128)S(1)} %bitcast_add_fusion.3) | copy-start | bytes 3538948 | tf_op jit(solution)/shard_map/while
  119.7 2.1 %copy-start.8 = (f32[3,768]{1,0:T(4,128)}, f32[3,768]{1,0:T(4,128)S(1)}, u32[]{:S(2)}) copy-start(f32[3,768]{1,0:T(4,128)S(1)} %add_add_fusion.2) | copy-start | bytes 27652 | tf_op jit(solution)/shard_map/while
  121.8 18.0 %collective-permute-start.1 = (bf16[2,768,384]{1,2,0:T(8,128)(2,1)}, bf16[2,768,384]{1,2,0:T(8,128)(2,1)S(1)}, u32[]{:S(2)}, u32[]{:S(2)}) collective-permute-start(bf16[2,768,384]{1,2,0:T(8,128)(2,1)} %get-tuple-element.328), channel_id=1, source_target_pairs={{16,0},{32,16},{48,32},{64,48},{80,64},{96,80},{112,96},{128,112},... | collective-permute-start | bytes 3538952 | tf_op jit(solution)/shard_map/while/body/ppermute | solution.py:13
  123.7 19.7 %collective-permute-start = (bf16[2,768,384]{1,2,0:T(8,128)(2,1)}, bf16[2,768,384]{1,2,0:T(8,128)(2,1)S(1)}, u32[]{:S(2)}, u32[]{:S(2)}) collective-permute-start(bf16[2,768,384]{1,2,0:T(8,128)(2,1)} %get-tuple-element.329), channel_id=1, source_target_pairs={{0,16},{16,32},{32,48},{48,64},{64,80},{80,96},{96,112},{112,128},... | collective-permute-start | bytes 3538952 | tf_op jit(solution)/shard_map/while/body/ppermute | solution.py:13
  130.5 9.4 %copy-start.3 = (pred[768,768]{0,1:T(8,128)(4,1)S(1)}, pred[768,768]{0,1:T(8,128)(4,1)}, u32[]{:S(2)}) copy-start(pred[768,768]{0,1:T(8,128)(4,1)} %copy.76) | copy-start | bytes 1769476 | tf_op jit(solution)/shard_map/while
  130.6 9.4 %copy-start.6 = (bf16[1,768,384]{1,2,0:T(8,128)(2,1)S(1)}, bf16[1,768,384]{1,2,0:T(8,128)(2,1)}, u32[]{:S(2)}) copy-start(bf16[1,768,384]{1,2,0:T(8,128)(2,1)} %get-tuple-element.347) | copy-start | bytes 1769476 | tf_op jit(solution)/shard_map/while
  145.5 1.6 copy-start.1
  147.0 0.7 copy-start.7
  147.4 2.5 %copy-start.2 = (f32[768,384]{0,1:T(8,128)}, f32[768,384]{0,1:T(8,128)S(1)}, u32[]{:S(2)}) copy-start(f32[768,384]{0,1:T(8,128)S(1)} %bitcast_add_fusion.3) | copy-start | bytes 3538948 | tf_op jit(solution)/shard_map/while
  147.8 2.1 %copy-start.8 = (f32[3,768]{1,0:T(4,128)}, f32[3,768]{1,0:T(4,128)S(1)}, u32[]{:S(2)}) copy-start(f32[3,768]{1,0:T(4,128)S(1)} %add_add_fusion.2) | copy-start | bytes 27652 | tf_op jit(solution)/shard_map/while
  149.8 18.0 %collective-permute-start.1 = (bf16[2,768,384]{1,2,0:T(8,128)(2,1)}, bf16[2,768,384]{1,2,0:T(8,128)(2,1)S(1)}, u32[]{:S(2)}, u32[]{:S(2)}) collective-permute-start(bf16[2,768,384]{1,2,0:T(8,128)(2,1)} %get-tuple-element.328), channel_id=1, source_target_pairs={{16,0},{32,16},{48,32},{64,48},{80,64},{96,80},{112,96},{128,112},... | collective-permute-start | bytes 3538952 | tf_op jit(solution)/shard_map/while/body/ppermute | solution.py:13
  151.8 19.7 %collective-permute-start = (bf16[2,768,384]{1,2,0:T(8,128)(2,1)}, bf16[2,768,384]{1,2,0:T(8,128)(2,1)S(1)}, u32[]{:S(2)}, u32[]{:S(2)}) collective-permute-start(bf16[2,768,384]{1,2,0:T(8,128)(2,1)} %get-tuple-element.329), channel_id=1, source_target_pairs={{0,16},{16,32},{32,48},{48,64},{64,80},{80,96},{96,112},{112,128},... | collective-permute-start | bytes 3538952 | tf_op jit(solution)/shard_map/while/body/ppermute | solution.py:13
  158.6 9.4 %copy-start.3 = (pred[768,768]{0,1:T(8,128)(4,1)S(1)}, pred[768,768]{0,1:T(8,128)(4,1)}, u32[]{:S(2)}) copy-start(pred[768,768]{0,1:T(8,128)(4,1)} %copy.76) | copy-start | bytes 1769476 | tf_op jit(solution)/shard_map/while
  158.6 9.4 %copy-start.6 = (bf16[1,768,384]{1,2,0:T(8,128)(2,1)S(1)}, bf16[1,768,384]{1,2,0:T(8,128)(2,1)}, u32[]{:S(2)}) copy-start(bf16[1,768,384]{1,2,0:T(8,128)(2,1)} %get-tuple-element.347) | copy-start | bytes 1769476 | tf_op jit(solution)/shard_map/while
  173.5 1.6 copy-start.1
  175.1 0.7 copy-start.7
  175.4 2.5 %copy-start.2 = (f32[768,384]{0,1:T(8,128)}, f32[768,384]{0,1:T(8,128)S(1)}, u32[]{:S(2)}) copy-start(f32[768,384]{0,1:T(8,128)S(1)} %bitcast_add_fusion.3) | copy-start | bytes 3538948 | tf_op jit(solution)/shard_map/while
  175.8 2.1 %copy-start.8 = (f32[3,768]{1,0:T(4,128)}, f32[3,768]{1,0:T(4,128)S(1)}, u32[]{:S(2)}) copy-start(f32[3,768]{1,0:T(4,128)S(1)} %add_add_fusion.2) | copy-start | bytes 27652 | tf_op jit(solution)/shard_map/while
Sparse Core Ops, SparseCore 0:
  9.1 57.1 all-gather.1
where the time goes:
time: 201 us; the launch traced here: 200 us
  waiting for transfers between devices  67.7 us (34%)
  matrix products  41.3 us (21%)
  blocking collectives  24.7 us (12%)
  local copies, waits for them, and re-layouts  24 us (12%)
  starting transfers between devices  16.9 us (8%)
  between operations  14.7 us (7%)
  other arithmetic  10.2 us (5%)
    all_gather x1, waiting for transfers between devices, shards(): piece = lax.all_gather(hidden, 'head', axis=0, tiled=True)  39.2 us
    ppermute x6, waiting for transfers between devices, shifted(): return lax.ppermute(block, axis, route)  27.8 us
    ppermute x6, starting transfers between devices, shifted(): return lax.ppermute(block, axis, route)  16.9 us
    dot_general x3, matrix products, shards(): jnp.dot(piece, qkv_weight[j], preferred_element_type=jnp.float32)  15.3 us
    dot_general x7, matrix products, tile_terms(): jnp.einsum('qhd,khd->hqk', query_h, keys_h, preferred_element_type=jnp.fl...  14 us
    all_to_all x1, blocking collectives, shards(): lax.all_to_all(attended, 'head', split_axis=0, concat_axis=1, tiled=True)  12.7 us
    pmax x1, blocking collectives, shards(): farthest = lax.pmax(jnp.stack([ahead, behind]), 'blk')  12 us
    dot_general x7, matrix products, tile_terms(): jnp.einsum('hqk,khd->qhd', weights.astype(jnp.bfloat16), values_h, prefer...  11.9 us
  transfers between devices with their start and end apart: 7, of which 4 were waited for; matrix products, arithmetic and copies ran while one was open for 13% of the time, Pallas kernels for 0%

commit v1 on v0

--- a/solution.py
+++ b/solution.py
@@ -60,7 +60,9 @@
 
 def shards(hidden, qkv_weight, qkv_bias, norm_gains, tile_lists, tile_counts):
     heads = qkv_weight.shape[2] // HD
-    piece = lax.all_gather(hidden, "head", axis=0, tiled=True)
+    piece = jnp.concatenate(
+        lax.all_to_all(jnp.stack([hidden] * lax.axis_size("head")), "head", 0, 0), axis=0
+    )
     made = [
         jnp.dot(piece, qkv_weight[j], preferred_element_type=jnp.float32)
         + qkv_bias[j].astype(jnp.float32)

time: 201 us -> 191 us (0.950)
  between operations: 14.7 us -> 1.46 us
  waiting for transfers between devices: 67.7 us -> 61.5 us
  starting transfers between devices: 16.9 us -> 23 us
  local copies, waits for them, and re-layouts: 24 us -> 27.4 us
    all_gather x1 -> x0, waiting for transfers between devices: 39.2 us -> none  [shards(): piece = lax.all_gather(hidden, 'head', axis=0, tiled=True)]
    all_to_all x0 -> x1, waiting for transfers between devices: none -> 33.6 us  [shards(): lax.all_to_all(jnp.stack([hidden] * lax.axis_size('head')), 'head', 0, 0)]
    all_to_all x0 -> x1, starting transfers between devices: none -> 5.06 us  [shards(): lax.all_to_all(jnp.stack([hidden] * lax.axis_size('head')), 'head', 0, 0)]
    another operation x0 -> x1, local copies, waits for them, and re-layouts: none -> 4.04 us  [shards(): jnp.stack([hidden] * lax.axis_size('head'))]
    while x42 -> x48, local copies, waits for them, and re-layouts: 7.32 us -> 7.31 us
  transfers between devices with their start and end apart: 7 -> 7, of which waited for: 4 -> 4; matrix products, arithmetic and copies ran while one was open for 13% -> 14% of each run, Pallas kernels for 0% -> 0%
where the time goes in v1:
time: 191 us; the launch traced here: 189 us
  waiting for transfers between devices  61.5 us (32%)
  matrix products  41.7 us (22%)
  local copies, waits for them, and re-layouts  27.4 us (14%)
  blocking collectives  24.3 us (13%)
  starting transfers between devices  23 us (12%)
  other arithmetic  9.49 us (5%)
    all_to_all x1, waiting for transfers between devices, shards(): lax.all_to_all(jnp.stack([hidden] * lax.axis_size('head')), 'head', 0, 0)  33.6 us
    ppermute x6, waiting for transfers between devices, shifted(): return lax.ppermute(block, axis, route)  27.8 us
    ppermute x6, starting transfers between devices, shifted(): return lax.ppermute(block, axis, route)  18 us
    dot_general x3, matrix products, shards(): jnp.dot(piece, qkv_weight[j], preferred_element_type=jnp.float32)  15.3 us
    dot_general x7, matrix products, tile_terms(): jnp.einsum('qhd,khd->hqk', query_h, keys_h, preferred_element_type=jnp.fl...  14.2 us
    pmax x1, blocking collectives, shards(): farthest = lax.pmax(jnp.stack([ahead, behind]), 'blk')  12.8 us
    dot_general x7, matrix products, tile_terms(): jnp.einsum('hqk,khd->qhd', weights.astype(jnp.bfloat16), values_h, prefer...  12.2 us
    all_to_all x1, blocking collectives, shards(): lax.all_to_all(attended, 'head', split_axis=0, concat_axis=1, tiled=True)  11.4 us
  transfers between devices with their start and end apart: 7, of which 4 were waited for; matrix products, arithmetic and copies ran while one was open for 14% of the time, Pallas kernels for 0%

profile of v1, /device:TPU:65, one launch (start us, length us, event | category | flops | bytes accessed | tf_op | source)
XLA Modules:
  0.0 189.3 jit_solution(1933894426212886928)
XLA Ops:
  0.0 4.0 %stack.24 = bf16[4,192,3072]{2,1,0:T(8,128)(2,1)} broadcast(bf16[192,3072]{1,0:T(8,128)(2,1)} %param.8), dimensions={1,2} | broadcast | bytes 5898240 | tf_op jit(solution)/shard_map/stack | solution.py:64
  4.0 5.1 %all-to-all-start = ((bf16[4,192,3072]{2,1,0:T(8,128)(2,1)}), bf16[4,192,3072]{2,1,0:T(8,128)(2,1)}, u32[]{:S(2)}, u32[]{:S(2)}) async-start(bf16[4,192,3072]{2,1,0:T(8,128)(2,1)} %stack.24), calls=%async_computation | async-start | bytes 9437184 | tf_op jit(solution)/shard_map/all_to_all | solution.py:64
  11.4 12.8 %pmax.7 = s32[2]{0:T(128)S(1)} all-reduce(s32[2]{0:T(128)S(1)} %pad_add_fusion), channel_id=1, replica_groups=mesh['blk'=16,'head'=4,'dp'=4] {'blk'}, use_global_device_ids=true, to_apply=%region_6.7 | all-reduce | flops 2 | bytes 16 | tf_op jit(solution)/shard_map/pmax | solution.py:89
  29.4 33.6 %all-to-all-done = bf16[4,192,3072]{2,1,0:T(8,128)(2,1)} async-done(((bf16[4,192,3072]{2,1,0:T(8,128)(2,1)}), bf16[4,192,3072]{2,1,0:T(8,128)(2,1)}, u32[]{:S(2)}, u32[]{:S(2)}) %all-to-all-start) | async-done | bytes 4718624 | tf_op jit(solution)/shard_map/all_to_all | solution.py:64
  63.0 5.1 %fusion.60 = (f32[768,384]{0,1:T(8,128)S(1)}, f32[768,384]{0,1:T(8,128)S(1)}) fusion(f32[384]{0:T(512)S(1)} %get-tuple-element.181, bf16[768,3072]{1,0:T(8,128)(2,1)} %bitcast.12, bf16[3,3072,384]{2,1,0:T(8,128)(2,1)} %param.9), kind=kOutput, calls=%fused_computation.93 | convolution fusion | flops 1812529152 | bytes 9438720 | tf_op jit(solution)/shard_map/dot_general | solution.py:67
  68.9 5.1 %fusion.59 = (f32[768,384]{0,1:T(8,128)S(1)}, f32[768,384]{0,1:T(8,128)S(1)}) fusion(f32[384]{0:T(512)} %get-tuple-element.180, bf16[768,3072]{1,0:T(8,128)(2,1)} %bitcast.12, bf16[3,3072,384]{2,1,0:T(8,128)(2,1)} %param.9), kind=kOutput, calls=%fused_computation.92 | convolution fusion | flops 1812529152 | bytes 9439232 | tf_op jit(solution)/shard_map/dot_general | solution.py:67
  75.4 5.1 %fusion.45 = bf16[768,384]{0,1:T(8,128)(2,1)S(1)} fusion(bf16[768,3072]{1,0:T(8,128)(2,1)} %bitcast.12, bf16[3,3072,384]{2,1,0:T(8,128)(2,1)} %param.9, f32[384]{0:T(512)} %get-tuple-element.179), kind=kOutput, calls=%fused_computation.53 | convolution fusion | flops 1812529152 | bytes 7669760 | tf_op jit(solution)/shard_map/dot_general | solution.py:67
  81.8 2.5 %copy.81 = bf16[2,768,384]{1,2,0:T(8,128)(2,1)} copy(bf16[2,768,384]{1,2,0:T(8,128)(2,1)} %pad_maximum_fusion) | data formatting | bytes 2359296
  84.5 2.5 %fusion.21 = (f32[3,768]{1,0:T(4,128)}, f32[3,768,768]{1,2,0:T(8,128)S(1)}) fusion(pred[768,768]{0,1:T(8,128)(4,1)S(1)} %copy-done.4, bf16[768,3,128]{0,2,1:T(8,128)(2,1)S(1)} %bitcast.139, bf16[768,3,128]{0,2,1:T(8,128)(2,1)S(1)} %bitcast.136), kind=kOutput, calls=%fused_computation.36 | convolution fusion | flops 458290944 | bytes 8856576 | tf_op jit(solution)/shard_map/qhd,khd->hqk/dot_general | solution.py:36
  87.0 2.6 %fusion.22 = f32[3,128,768]{2,1,0:T(8,128)} fusion(bf16[768,3,128]{0,2,1:T(8,128)(2,1)S(1)} %bitcast.144, f32[3,768,768]{1,2,0:T(8,128)S(1)} %get-tuple-element.223, pred[768,768]{0,1:T(8,128)(4,1)S(1)} %copy-done.4), kind=kOutput, calls=%fused_computation.37 | convolution fusion | flops 458293248 | bytes 9437184 | tf_op jit(solution)/shard_map/hqk,khd->qhd/dot_general | solution.py:44
  89.6 85.8 %while.19 = (s32[]{:T(128)}, f32[3,768]{1,0:T(4,128)}, f32[768,384]{0,1:T(8,128)}, bf16[2,768,384]{1,2,0:T(8,128)(2,1)}, bf16[2,768,384]{1,2,0:T(8,128)(2,1)}, /...) while((s32[]{:T(128)}, f32[3,768]{1,0:T(4,128)}, ...), condition=%wide.region_12.13_spmd, body=%wide.region_7.12_spmd.sunk | while | flops 1833884160 | bytes 78004888 | solution.py:105
  89.6 3.4 %collective-permute-start.1 = (bf16[2,768,384]{1,2,0:T(8,128)(2,1)}, bf16[2,768,384]{1,2,0:T(8,128)(2,1)S(1)}, u32[]{:S(2)}, u32[]{:S(2)}) collective-permute-start(bf16[2,768,384]{1,2,0:T(8,128)(2,1)} %get-tuple-element.328), channel_id=1, source_target_pairs={{16,0},{32,16},{48,32},{64,48},{80,64},{96,80},{112,96},{128,112},... | collective-permute-start | bytes 3538952 | tf_op jit(solution)/shard_map/while/body/ppermute | solution.py:13
  93.0 3.4 %collective-permute-start = (bf16[2,768,384]{1,2,0:T(8,128)(2,1)}, bf16[2,768,384]{1,2,0:T(8,128)(2,1)S(1)}, u32[]{:S(2)}, u32[]{:S(2)}) collective-permute-start(bf16[2,768,384]{1,2,0:T(8,128)(2,1)} %get-tuple-element.329), channel_id=1, source_target_pairs={{0,16},{16,32},{32,48},{48,64},{64,80},{80,96},{96,112},{112,128},... | collective-permute-start | bytes 3538952 | tf_op jit(solution)/shard_map/while/body/ppermute | solution.py:13
  99.7 9.3 %collective-permute-done.1 = bf16[2,768,384]{1,2,0:T(8,128)(2,1)S(1)} collective-permute-done((bf16[2,768,384]{1,2,0:T(8,128)(2,1)}, bf16[2,768,384]{1,2,0:T(8,128)(2,1)S(1)}, u32[]{:S(2)}, u32[]{:S(2)}) %collective-permute-start.1) | collective-permute-done | bytes 1179680 | tf_op jit(solution)/shard_map/while/body/ppermute | solution.py:13
  109.0 2.0 %fusion.98 = (f32[3,768]{1,0:T(4,128)S(1)}, f32[3,768,768]{1,2,0:T(8,128)S(1)}) fusion(pred[768,768]{0,1:T(8,128)(4,1)S(1)} %copy-done.3, bf16[768,3,128]{0,2,1:T(8,128)(2,1)S(1)} %bitcast.141, bf16[768,3,128]{0,2,1:T(8,128)(2,1)S(1)} %bitcast.130), kind=kOutput, calls=%fused_computation.3.clone.1 | convolution fusion | flops 458290944 | bytes 8856576 | tf_op jit(solution)/shard_map/while/body/qhd,khd->hqk/dot_general | solution.py:36
  111.0 1.6 fusion.100
  112.7 1.9 %fusion.96 = (f32[3,768]{1,0:T(4,128)S(1)}, f32[3,768,768]{1,2,0:T(8,128)S(1)}) fusion(pred[768,768]{0,1:T(8,128)(4,1)S(1)} %copy.75, bf16[768,3,128]{0,2,1:T(8,128)(2,1)S(1)} %bitcast.142, bf16[768,3,128]{0,2,1:T(8,128)(2,1)S(1)} %bitcast.131), kind=kOutput, calls=%fused_computation.5.clone.1 | convolution fusion | flops 458290944 | bytes 8856576 | tf_op jit(solution)/shard_map/while/body/qhd,khd->hqk/dot_general | solution.py:36
  119.0 1.9 %collective-permute-start.1 = (bf16[2,768,384]{1,2,0:T(8,128)(2,1)}, bf16[2,768,384]{1,2,0:T(8,128)(2,1)S(1)}, u32[]{:S(2)}, u32[]{:S(2)}) collective-permute-start(bf16[2,768,384]{1,2,0:T(8,128)(2,1)} %get-tuple-element.328), channel_id=1, source_target_pairs={{16,0},{32,16},{48,32},{64,48},{80,64},{96,80},{112,96},{128,112},... | collective-permute-start | bytes 3538952 | tf_op jit(solution)/shard_map/while/body/ppermute | solution.py:13
  121.0 3.6 %collective-permute-start = (bf16[2,768,384]{1,2,0:T(8,128)(2,1)}, bf16[2,768,384]{1,2,0:T(8,128)(2,1)S(1)}, u32[]{:S(2)}, u32[]{:S(2)}) collective-permute-start(bf16[2,768,384]{1,2,0:T(8,128)(2,1)} %get-tuple-element.329), channel_id=1, source_target_pairs={{0,16},{16,32},{32,48},{48,64},{64,80},{80,96},{96,112},{112,128},... | collective-permute-start | bytes 3538952 | tf_op jit(solution)/shard_map/while/body/ppermute | solution.py:13
  127.8 9.3 %collective-permute-done.1 = bf16[2,768,384]{1,2,0:T(8,128)(2,1)S(1)} collective-permute-done((bf16[2,768,384]{1,2,0:T(8,128)(2,1)}, bf16[2,768,384]{1,2,0:T(8,128)(2,1)S(1)}, u32[]{:S(2)}, u32[]{:S(2)}) %collective-permute-start.1) | collective-permute-done | bytes 1179680 | tf_op jit(solution)/shard_map/while/body/ppermute | solution.py:13
  137.2 2.0 %fusion.98 = (f32[3,768]{1,0:T(4,128)S(1)}, f32[3,768,768]{1,2,0:T(8,128)S(1)}) fusion(pred[768,768]{0,1:T(8,128)(4,1)S(1)} %copy-done.3, bf16[768,3,128]{0,2,1:T(8,128)(2,1)S(1)} %bitcast.141, bf16[768,3,128]{0,2,1:T(8,128)(2,1)S(1)} %bitcast.130), kind=kOutput, calls=%fused_computation.3.clone.1 | convolution fusion | flops 458290944 | bytes 8856576 | tf_op jit(solution)/shard_map/while/body/qhd,khd->hqk/dot_general | solution.py:36
  139.1 1.6 fusion.100
  140.9 1.9 %fusion.96 = (f32[3,768]{1,0:T(4,128)S(1)}, f32[3,768,768]{1,2,0:T(8,128)S(1)}) fusion(pred[768,768]{0,1:T(8,128)(4,1)S(1)} %copy.75, bf16[768,3,128]{0,2,1:T(8,128)(2,1)S(1)} %bitcast.142, bf16[768,3,128]{0,2,1:T(8,128)(2,1)S(1)} %bitcast.131), kind=kOutput, calls=%fused_computation.5.clone.1 | convolution fusion | flops 458290944 | bytes 8856576 | tf_op jit(solution)/shard_map/while/body/qhd,khd->hqk/dot_general | solution.py:36
  142.8 1.6 fusion.99
  147.2 1.9 %collective-permute-start.1 = (bf16[2,768,384]{1,2,0:T(8,128)(2,1)}, bf16[2,768,384]{1,2,0:T(8,128)(2,1)S(1)}, u32[]{:S(2)}, u32[]{:S(2)}) collective-permute-start(bf16[2,768,384]{1,2,0:T(8,128)(2,1)} %get-tuple-element.328), channel_id=1, source_target_pairs={{16,0},{32,16},{48,32},{64,48},{80,64},{96,80},{112,96},{128,112},... | collective-permute-start | bytes 3538952 | tf_op jit(solution)/shard_map/while/body/ppermute | solution.py:13
  149.1 3.6 %collective-permute-start = (bf16[2,768,384]{1,2,0:T(8,128)(2,1)}, bf16[2,768,384]{1,2,0:T(8,128)(2,1)S(1)}, u32[]{:S(2)}, u32[]{:S(2)}) collective-permute-start(bf16[2,768,384]{1,2,0:T(8,128)(2,1)} %get-tuple-element.329), channel_id=1, source_target_pairs={{0,16},{16,32},{32,48},{48,64},{64,80},{80,96},{96,112},{112,128},... | collective-permute-start | bytes 3538952 | tf_op jit(solution)/shard_map/while/body/ppermute | solution.py:13
  155.9 9.3 %collective-permute-done.1 = bf16[2,768,384]{1,2,0:T(8,128)(2,1)S(1)} collective-permute-done((bf16[2,768,384]{1,2,0:T(8,128)(2,1)}, bf16[2,768,384]{1,2,0:T(8,128)(2,1)S(1)}, u32[]{:S(2)}, u32[]{:S(2)}) %collective-permute-start.1) | collective-permute-done | bytes 1179680 | tf_op jit(solution)/shard_map/while/body/ppermute | solution.py:13
  165.3 2.0 %fusion.98 = (f32[3,768]{1,0:T(4,128)S(1)}, f32[3,768,768]{1,2,0:T(8,128)S(1)}) fusion(pred[768,768]{0,1:T(8,128)(4,1)S(1)} %copy-done.3, bf16[768,3,128]{0,2,1:T(8,128)(2,1)S(1)} %bitcast.141, bf16[768,3,128]{0,2,1:T(8,128)(2,1)S(1)} %bitcast.130), kind=kOutput, calls=%fused_computation.3.clone.1 | convolution fusion | flops 458290944 | bytes 8856576 | tf_op jit(solution)/shard_map/while/body/qhd,khd->hqk/dot_general | solution.py:36
  167.3 1.6 fusion.100
  169.0 1.9 %fusion.96 = (f32[3,768]{1,0:T(4,128)S(1)}, f32[3,768,768]{1,2,0:T(8,128)S(1)}) fusion(pred[768,768]{0,1:T(8,128)(4,1)S(1)} %copy.75, bf16[768,3,128]{0,2,1:T(8,128)(2,1)S(1)} %bitcast.142, bf16[768,3,128]{0,2,1:T(8,128)(2,1)S(1)} %bitcast.131), kind=kOutput, calls=%fused_computation.5.clone.1 | convolution fusion | flops 458290944 | bytes 8856576 | tf_op jit(solution)/shard_map/while/body/qhd,khd->hqk/dot_general | solution.py:36
  170.9 1.6 fusion.99
  177.0 11.4 %all_to_all.24 = bf16[4,192,384]{2,1,0:T(8,128)(2,1)S(1)} all-to-all(bf16[4,192,384]{2,1,0:T(8,128)(2,1)S(1)} %bitcast.133), channel_id=1, replica_groups=mesh['blk'=16,'head'=4,'dp'=4] {'head'}, dimensions={0} | all-to-all | bytes 1179648 | tf_op jit(solution)/shard_map/all_to_all | solution.py:112
  (129 shorter events, 32.0 us)
Async XLA Ops:
  0.0 9.1 %copy-start = (s32[32,12]{0,1:T(8,128)S(1)}, s32[32,12]{0,1:T(8,128)}, u32[]{:S(2)}) copy-start(s32[32,12]{0,1:T(8,128)} %param.12) | copy-start | bytes 4612
  4.0 5.3 %copy-start.16 = (s32[32]{0:T(128)S(1)}, s32[32]{0:T(128)}, u32[]{:S(2)}) copy-start(s32[32]{0:T(128)} %param.13) | copy-start | bytes 388
  4.0 24.1 %copy-start.11 = (bf16[3,384]{1,0:T(4,128)(2,1)S(1)}, bf16[3,384]{1,0:T(4,128)(2,1)}, u32[]{:S(2)}) copy-start(bf16[3,384]{1,0:T(4,128)(2,1)} %param.10) | copy-start | bytes 6916
  4.0 24.7 %copy-start.12 = (f32[2,128]{1,0:T(2,128)S(1)}, f32[2,128]{1,0:T(2,128)}, u32[]{:S(2)}) copy-start(f32[2,128]{1,0:T(2,128)} %param.11) | copy-start | bytes 3076
  4.0 59.0 %all-to-all-start = ((bf16[4,192,3072]{2,1,0:T(8,128)(2,1)}), bf16[4,192,3072]{2,1,0:T(8,128)(2,1)}, u32[]{:S(2)}, u32[]{:S(2)}) async-start(bf16[4,192,3072]{2,1,0:T(8,128)(2,1)} %stack.24), calls=%async_computation | async-start | bytes 9437184 | tf_op jit(solution)/shard_map/all_to_all | solution.py:64
  9.4 15.0 %copy-start.13 = (s32[2]{0:T(128)}, s32[2]{0:T(128)S(1)}, u32[]{:S(2)}) copy-start(s32[2]{0:T(128)S(1)} %dynamic_slice.7) | copy-start | bytes 28
  75.4 5.1 %copy-start.9 = (f32[768,3]{0,1:T(4,128)S(1)}, f32[768,3]{0,1:T(4,128)}, u32[]{:S(2)}) copy-start(f32[768,3]{0,1:T(4,128)} %add_rsqrt_fusion) | copy-start | bytes 27652
  75.4 5.1 %copy-start.10 = (f32[384]{0:T(512)S(1)}, f32[384]{0:T(512)}, u32[]{:S(2)}) copy-start(f32[384]{0:T(512)} %get-tuple-element.224) | copy-start | bytes 4612
  81.8 2.7 %copy-start.4 = (pred[768,768]{0,1:T(8,128)(4,1)S(1)}, pred[768,768]{0,1:T(8,128)(4,1)}, u32[]{:S(2)}) copy-start(pred[768,768]{0,1:T(8,128)(4,1)} %copy.56) | copy-start | bytes 1769476
  84.5 2.5 %copy-start.5 = (bf16[768,384]{0,1:T(8,128)(2,1)}, bf16[768,384]{0,1:T(8,128)(2,1)S(1)}, u32[]{:S(2)}) copy-start(bf16[768,384]{0,1:T(8,128)(2,1)S(1)} %fusion.52) | copy-start | bytes 1769476
  87.0 2.6 %copy-start.14 = (s32[2]{0:T(128)S(1)}, s32[2]{0:T(128)}, u32[]{:S(2)}) copy-start(s32[2]{0:T(128)} %copy-done.13) | copy-start | bytes 28
  89.6 19.3 %collective-permute-start.1 = (bf16[2,768,384]{1,2,0:T(8,128)(2,1)}, bf16[2,768,384]{1,2,0:T(8,128)(2,1)S(1)}, u32[]{:S(2)}, u32[]{:S(2)}) collective-permute-start(bf16[2,768,384]{1,2,0:T(8,128)(2,1)} %get-tuple-element.328), channel_id=1, source_target_pairs={{16,0},{32,16},{48,32},{64,48},{80,64},{96,80},{112,96},{128,112},... | collective-permute-start | bytes 3538952 | tf_op jit(solution)/shard_map/while/body/ppermute | solution.py:13
  93.0 19.6 %collective-permute-start = (bf16[2,768,384]{1,2,0:T(8,128)(2,1)}, bf16[2,768,384]{1,2,0:T(8,128)(2,1)S(1)}, u32[]{:S(2)}, u32[]{:S(2)}) collective-permute-start(bf16[2,768,384]{1,2,0:T(8,128)(2,1)} %get-tuple-element.329), channel_id=1, source_target_pairs={{0,16},{16,32},{32,48},{48,64},{64,80},{80,96},{96,112},{112,128},... | collective-permute-start | bytes 3538952 | tf_op jit(solution)/shard_map/while/body/ppermute | solution.py:13
  99.6 9.4 %copy-start.3 = (pred[768,768]{0,1:T(8,128)(4,1)S(1)}, pred[768,768]{0,1:T(8,128)(4,1)}, u32[]{:S(2)}) copy-start(pred[768,768]{0,1:T(8,128)(4,1)} %copy.76) | copy-start | bytes 1769476 | tf_op jit(solution)/shard_map/while
  99.6 9.4 %copy-start.6 = (bf16[1,768,384]{1,2,0:T(8,128)(2,1)S(1)}, bf16[1,768,384]{1,2,0:T(8,128)(2,1)}, u32[]{:S(2)}) copy-start(bf16[1,768,384]{1,2,0:T(8,128)(2,1)} %get-tuple-element.347) | copy-start | bytes 1769476 | tf_op jit(solution)/shard_map/while
  116.6 2.5 %copy-start.2 = (f32[768,384]{0,1:T(8,128)}, f32[768,384]{0,1:T(8,128)S(1)}, u32[]{:S(2)}) copy-start(f32[768,384]{0,1:T(8,128)S(1)} %bitcast_add_fusion.3) | copy-start | bytes 3538948 | tf_op jit(solution)/shard_map/while
  117.0 2.1 %copy-start.8 = (f32[3,768]{1,0:T(4,128)}, f32[3,768]{1,0:T(4,128)S(1)}, u32[]{:S(2)}) copy-start(f32[3,768]{1,0:T(4,128)S(1)} %add_add_fusion.2) | copy-start | bytes 27652 | tf_op jit(solution)/shard_map/while
  117.0 2.1 %copy-start.15 = (s32[2]{0:T(128)S(1)}, s32[2]{0:T(128)}, u32[]{:S(2)}) copy-start(s32[2]{0:T(128)} %get-tuple-element.368) | copy-start | bytes 28 | tf_op jit(solution)/shard_map/while
  119.0 18.0 %collective-permute-start.1 = (bf16[2,768,384]{1,2,0:T(8,128)(2,1)}, bf16[2,768,384]{1,2,0:T(8,128)(2,1)S(1)}, u32[]{:S(2)}, u32[]{:S(2)}) collective-permute-start(bf16[2,768,384]{1,2,0:T(8,128)(2,1)} %get-tuple-element.328), channel_id=1, source_target_pairs={{16,0},{32,16},{48,32},{64,48},{80,64},{96,80},{112,96},{128,112},... | collective-permute-start | bytes 3538952 | tf_op jit(solution)/shard_map/while/body/ppermute | solution.py:13
  121.0 19.8 %collective-permute-start = (bf16[2,768,384]{1,2,0:T(8,128)(2,1)}, bf16[2,768,384]{1,2,0:T(8,128)(2,1)S(1)}, u32[]{:S(2)}, u32[]{:S(2)}) collective-permute-start(bf16[2,768,384]{1,2,0:T(8,128)(2,1)} %get-tuple-element.329), channel_id=1, source_target_pairs={{0,16},{16,32},{32,48},{48,64},{64,80},{80,96},{96,112},{112,128},... | collective-permute-start | bytes 3538952 | tf_op jit(solution)/shard_map/while/body/ppermute | solution.py:13
  127.8 9.4 %copy-start.3 = (pred[768,768]{0,1:T(8,128)(4,1)S(1)}, pred[768,768]{0,1:T(8,128)(4,1)}, u32[]{:S(2)}) copy-start(pred[768,768]{0,1:T(8,128)(4,1)} %copy.76) | copy-start | bytes 1769476 | tf_op jit(solution)/shard_map/while
  127.8 9.4 %copy-start.6 = (bf16[1,768,384]{1,2,0:T(8,128)(2,1)S(1)}, bf16[1,768,384]{1,2,0:T(8,128)(2,1)}, u32[]{:S(2)}) copy-start(bf16[1,768,384]{1,2,0:T(8,128)(2,1)} %get-tuple-element.347) | copy-start | bytes 1769476 | tf_op jit(solution)/shard_map/while
  144.7 2.5 %copy-start.2 = (f32[768,384]{0,1:T(8,128)}, f32[768,384]{0,1:T(8,128)S(1)}, u32[]{:S(2)}) copy-start(f32[768,384]{0,1:T(8,128)S(1)} %bitcast_add_fusion.3) | copy-start | bytes 3538948 | tf_op jit(solution)/shard_map/while
  145.1 2.1 %copy-start.8 = (f32[3,768]{1,0:T(4,128)}, f32[3,768]{1,0:T(4,128)S(1)}, u32[]{:S(2)}) copy-start(f32[3,768]{1,0:T(4,128)S(1)} %add_add_fusion.2) | copy-start | bytes 27652 | tf_op jit(solution)/shard_map/while
  145.1 2.1 %copy-start.15 = (s32[2]{0:T(128)S(1)}, s32[2]{0:T(128)}, u32[]{:S(2)}) copy-start(s32[2]{0:T(128)} %get-tuple-element.368) | copy-start | bytes 28 | tf_op jit(solution)/shard_map/while
  147.2 18.0 %collective-permute-start.1 = (bf16[2,768,384]{1,2,0:T(8,128)(2,1)}, bf16[2,768,384]{1,2,0:T(8,128)(2,1)S(1)}, u32[]{:S(2)}, u32[]{:S(2)}) collective-permute-start(bf16[2,768,384]{1,2,0:T(8,128)(2,1)} %get-tuple-element.328), channel_id=1, source_target_pairs={{16,0},{32,16},{48,32},{64,48},{80,64},{96,80},{112,96},{128,112},... | collective-permute-start | bytes 3538952 | tf_op jit(solution)/shard_map/while/body/ppermute | solution.py:13
  149.1 19.8 %collective-permute-start = (bf16[2,768,384]{1,2,0:T(8,128)(2,1)}, bf16[2,768,384]{1,2,0:T(8,128)(2,1)S(1)}, u32[]{:S(2)}, u32[]{:S(2)}) collective-permute-start(bf16[2,768,384]{1,2,0:T(8,128)(2,1)} %get-tuple-element.329), channel_id=1, source_target_pairs={{0,16},{16,32},{32,48},{48,64},{64,80},{80,96},{96,112},{112,128},... | collective-permute-start | bytes 3538952 | tf_op jit(solution)/shard_map/while/body/ppermute | solution.py:13
  155.9 9.4 %copy-start.3 = (pred[768,768]{0,1:T(8,128)(4,1)S(1)}, pred[768,768]{0,1:T(8,128)(4,1)}, u32[]{:S(2)}) copy-start(pred[768,768]{0,1:T(8,128)(4,1)} %copy.76) | copy-start | bytes 1769476 | tf_op jit(solution)/shard_map/while
  155.9 9.4 %copy-start.6 = (bf16[1,768,384]{1,2,0:T(8,128)(2,1)S(1)}, bf16[1,768,384]{1,2,0:T(8,128)(2,1)}, u32[]{:S(2)}) copy-start(bf16[1,768,384]{1,2,0:T(8,128)(2,1)} %get-tuple-element.347) | copy-start | bytes 1769476 | tf_op jit(solution)/shard_map/while
  172.9 2.5 %copy-start.2 = (f32[768,384]{0,1:T(8,128)}, f32[768,384]{0,1:T(8,128)S(1)}, u32[]{:S(2)}) copy-start(f32[768,384]{0,1:T(8,128)S(1)} %bitcast_add_fusion.3) | copy-start | bytes 3538948 | tf_op jit(solution)/shard_map/while
  173.3 2.1 %copy-start.8 = (f32[3,768]{1,0:T(4,128)}, f32[3,768]{1,0:T(4,128)S(1)}, u32[]{:S(2)}) copy-start(f32[3,768]{1,0:T(4,128)S(1)} %add_add_fusion.2) | copy-start | bytes 27652 | tf_op jit(solution)/shard_map/while
  173.3 2.1 %copy-start.15 = (s32[2]{0:T(128)S(1)}, s32[2]{0:T(128)}, u32[]{:S(2)}) copy-start(s32[2]{0:T(128)} %get-tuple-element.368) | copy-start | bytes 28 | tf_op jit(solution)/shard_map/while
  (6 other events, 6.9 us)
